TPU v7x, 512 devices: a whole 4x8x8 slice. The times are simulated.
512 devices in a mesh: hst: 128 (over z, y, core), local: 4 (over x).
Axes of the slice: x: 4, y: 8, z: 8, core: 2. Of those that a mesh axis runs over, the one named last changes fastest.
Arguments:
- grads: bfloat16 [128, 4, 16, 49152], P('hst', 'local'), may hold values from -1.25 to 1.25
- master: float32 [16, 49152], P('local', 'hst'), may hold values from -3 to 3
- moment_one: float32 [16, 49152], P('local', 'hst'), may hold values from -3 to 3
- moment_two: float32 [16, 49152], P('local', 'hst'), may hold values from 0.01 to 2
Outputs:
- grad_total: float32 [16, 49152], P('local', 'hst')
- new_master: float32 [16, 49152], P('local', 'hst')
- new_one: float32 [16, 49152], P('local', 'hst')
- new_two: float32 [16, 49152], P('local', 'hst')
- secondary: bfloat16 [16, 49152], P('local')
All inputs are finite; a program needn't handle non-finite values.
Results may differ from a plain program's by a relative error of at most 0.001.
Values may be sent and summed in bfloat16 or wider, within the bound.
A program may use at most 64 MiB of HBM per device.

v0:
```python
import jax
import jax.numpy as jnp
from jax import lax
from jax.sharding import PartitionSpec as P

beta_one = 0.9
beta_two = 0.95
learn_rate = 0.02
decay_rate = 0.1
epsilon = 1e-08
correct_one = 1.0 - (0.9**50) ** 2
correct_two = 1.0 - (0.95**50) ** 2


def local(grads, master, moment_one, moment_two):
    local_count = lax.axis_size("local")
    host_count = lax.axis_size("hst")
    gradient = grads[0, 0]
    total_rows = gradient.shape[0]
    total_cols = gradient.shape[1]
    row_block = total_rows // local_count
    col_block = total_cols // host_count
    pieces = lax.all_to_all(
        gradient.reshape(local_count, row_block, total_cols),
        "local",
        split_axis=0,
        concat_axis=0,
        tiled=True,
    )
    partial_sum = jnp.sum(pieces.astype(jnp.float32), axis=0)
    arrived = lax.all_to_all(
        partial_sum.reshape(row_block, host_count, col_block),
        "hst",
        split_axis=1,
        concat_axis=1,
        tiled=True,
    )
    grad_total = jnp.sum(arrived, axis=1)
    new_one = beta_one * moment_one + (1.0 - beta_one) * grad_total
    new_two = beta_two * moment_two + (1.0 - beta_two) * grad_total * grad_total
    update = new_one / correct_one / (jnp.sqrt(new_two / correct_two) + epsilon)
    new_master = master - learn_rate * (update + decay_rate * master)
    secondary = lax.all_gather(new_master.astype(jnp.bfloat16), "hst", axis=1, tiled=True)
    return (grad_total, new_master, new_one, new_two, secondary)


def solution(mesh):
    return jax.shard_map(
        local,
        mesh=mesh,
        in_specs=(
            P("hst", "local", None, None),
            P("local", "hst"),
            P("local", "hst"),
            P("local", "hst"),
        ),
        out_specs=(
            P("local", "hst"),
            P("local", "hst"),
            P("local", "hst"),
            P("local", "hst"),
            P("local", None),
        ),
        check_vma=False,
    )
```

profile of v0, /device:TPU:1, one launch (start us, length us, event | category | flops | bytes accessed | tf_op | source)
XLA Modules:
  0.0 122.6 jit_solution(15280396725466493104)
XLA Ops:
  0.6 1.7 %reshape_squeeze.3 = bf16[4,4,49152]{2,1,0:T(4,128)(2,1)S(1)} reshape(bf16[1,1,16,49152]{3,2,1,0:T(8,128)(2,1)} %param.4) | data formatting | bytes 3145728 | tf_op jit(solution)/shard_map/reshape;squeeze | solution.py:24
  2.4 20.8 %all_to_all.10 = bf16[4,4,49152]{2,1,0:T(4,128)(2,1)S(1)} all-to-all(bf16[4,4,49152]{2,1,0:T(4,128)(2,1)S(1)} %reshape_squeeze.3), channel_id=1, replica_groups=mesh['hst'=128,'local'=4] {'local'}, dimensions={0} | all-to-all | bytes 3145728 | tf_op jit(solution)/shard_map/all_to_all | solution.py:23
  23.2 0.8 convert_reduce_fusion
  24.0 0.0 copy-start.1
  24.0 0.0 copy-start.2
  24.0 0.0 copy-start.3
  24.0 48.3 %all_to_all.11 = f32[4,128,384]{2,0,1:T(4,128)S(1)} all-to-all(f32[4,128,384]{2,0,1:T(4,128)S(1)} %bitcast.3), channel_id=1, replica_groups=mesh['hst'=128,'local'=4] {'hst'}, dimensions={1} | all-to-all | bytes 1572864 | tf_op jit(solution)/shard_map/all_to_all | solution.py:31
  72.3 0.2 reduce_sum.19
  72.5 0.0 copy-done.1
  72.5 0.0 copy-done.2
  72.5 0.0 copy-done.3
  72.5 0.0 copy-start
  72.5 0.6 fusion.1
  73.1 48.7 %all_gather.3 = bf16[4,49152]{1,0:T(4,128)(2,1)S(1)} all-gather(bf16[4,384]{1,0:T(4,128)(2,1)S(1)} %get-tuple-element.5), channel_id=1, replica_groups=mesh['hst'=128,'local'=4] {'hst'}, dimensions={1}, use_global_device_ids=true | all-gather | bytes 396288 | tf_op jit(solution)/shard_map/all_gather | solution.py:43
  121.8 0.7 copy.10
  122.6 0.0 copy-done
Async XLA Ops:
  24.0 48.5 %copy-start.1 = (f32[4,384]{1,0:T(4,128)S(1)}, f32[4,384]{1,0:T(4,128)}, u32[]{:S(2)}) copy-start(f32[4,384]{1,0:T(4,128)} %param.5) | copy-start | bytes 18436
  24.0 48.5 %copy-start.2 = (f32[4,384]{1,0:T(4,128)S(1)}, f32[4,384]{1,0:T(4,128)}, u32[]{:S(2)}) copy-start(f32[4,384]{1,0:T(4,128)} %param.6) | copy-start | bytes 18436
  24.0 48.5 %copy-start.3 = (f32[4,384]{1,0:T(4,128)S(1)}, f32[4,384]{1,0:T(4,128)}, u32[]{:S(2)}) copy-start(f32[4,384]{1,0:T(4,128)} %param.7) | copy-start | bytes 18436
  72.5 50.1 %copy-start = (f32[4,384]{1,0:T(4,128)}, f32[4,384]{1,0:T(4,128)S(1)}, u32[]{:S(2)}) copy-start(f32[4,384]{1,0:T(4,128)S(1)} %reduce_sum.19) | copy-start | bytes 18436
where the time goes:
time: 123 us
  blocking collectives  118 us (96%)
  local copies, waits for them, and re-layouts  2.5 us (2%)
  other arithmetic  1.59 us (1%)
    all_gather x1, blocking collectives, local(): lax.all_gather(new_master.astype(jnp.bfloat16), 'hst', axis=1, tiled=True)  48.7 us
    all_to_all x1, blocking collectives, local(): lax.all_to_all(partial_sum.reshape(row_block, host_count, col_block), 'hs...  48.3 us
    all_to_all x1, blocking collectives, local(): lax.all_to_all(gradient.reshape(local_count, row_block, total_cols), 'loc...  20.8 us

commit v1 on v0

v1 whole, which is shorter than its diff:
```python
import functools

import jax
import jax.numpy as jnp
from jax import lax
from jax.experimental import pallas as pl
from jax.experimental.pallas import tpu as pltpu
from jax.sharding import PartitionSpec as P

beta_one = 0.9
beta_two = 0.95
learn_rate = 0.02
decay_rate = 0.1
epsilon = 1e-08
correct_one = 1.0 - (0.9**50) ** 2
correct_two = 1.0 - (0.95**50) ** 2

NX, NY, NZ, NC = 4, 8, 8, 2
PARTS, LANES = 3, 128
MESH = pl.DeviceIdType.MESH
SEMS = 101


def kernel(
    grads,
    master,
    moment_one,
    moment_two,
    total_out,
    master_out,
    one_out,
    two_out,
    gathered,
    own,
    peer,
    sum_z,
    sum_y,
    sum_x,
    half_z,
    full_z,
    half_y,
    full_y,
    half_x,
    full_x,
    mid_z,
    mid_y,
    mid_x,
    got_z,
    got_y,
    got_x,
    end_z,
    end_y,
    end_x,
    last_z,
    last_y,
    last_x,
    load_sem,
    send_sem,
    recv_sem,
):
    x = lax.axis_index("local")
    h = lax.axis_index("hst")
    z, y, c = h // (NY * NC), (h // NC) % NY, h % NC

    def device(dx=0, dy=0, dz=0, dc=0):
        there = (((z + dz) % NZ) * NY + (y + dy) % NY) * NC + (c + dc) % NC
        return {"hst": there, "local": (x + dx) % NX}

    taken = []

    def send(src, dst, to):
        slot = len(taken)
        copy = pltpu.make_async_remote_copy(
            src_ref=src,
            dst_ref=dst,
            send_sem=send_sem.at[slot],
            recv_sem=recv_sem.at[slot],
            device_id=to,
            device_id_type=MESH,
        )
        copy.start()
        taken.append(copy)
        return copy

    barrier = pltpu.get_barrier_semaphore()
    peers = [device(dc=1)]
    peers += [device(dx=k) for k in range(1, NX)]
    peers += [device(dy=k) for k in range(1, NY)]
    peers += [device(dz=k) for k in range(1, NZ)]
    for to in peers:
        pl.semaphore_signal(barrier, inc=1, device_id=to, device_id_type=MESH)
    loads = []
    for p in range(PARTS):
        load = pltpu.make_async_copy(
            grads.at[:, :, :, c, p], own.at[p], load_sem.at[p]
        )
        load.start()
        loads.append(load)
    pl.semaphore_wait(barrier, len(peers))

    pairs = [
        send(grads.at[:, :, :, 1 - c, p], peer.at[p], device(dc=1))
        for p in range(PARTS)
    ]

    def pair_sum(p, row, i, j):
        return own[p, row, i, j].astype(jnp.float32) + peer[p, row, i, j].astype(
            jnp.float32
        )

    def fill_z(i, carry):
        for j in range(NY):
            for row in range(2):
                sum_z[i, j, row] = pair_sum(0, row, i, j)
        return carry

    def fill_y(i, carry):
        for j in range(NY):
            for row in range(2):
                sum_y[j, i, row] = pair_sum(1, row, i, j)
        return carry

    def fill_x(i, carry):
        for j in range(NY):
            for row in range(2):
                both = pair_sum(2, row, i, j)
                sum_x[2 * row, i, j] = both[0:4]
                sum_x[2 * row + 1, i, j] = both[4:8]
        return carry

    class Ring:
        def __init__(self, sums, half, full, at, size, hop):
            self.sums, self.half, self.full = sums, half, full
            self.at, self.size, self.hop = at, size, hop
            self.flight = [None, None]

        def step(self, s):
            far = self.size // 2
            cut = self.sums.shape[1] // 2
            for way, sign in enumerate((1, -1)):
                to = self.hop(sign)
                chunk = (self.at + self.size + sign * (far - s)) % self.size
                lo = way * cut
                if s == 0:
                    self.flight[way] = send(
                        self.sums.at[chunk, pl.ds(lo, cut)], self.half.at[way], to
                    )
                    continue
                self.flight[way].wait_recv()
                if s == 1:
                    self.sums[chunk, pl.ds(lo, cut)] += self.half[way]
                else:
                    self.sums[chunk] += self.full[way, s - 2]
                self.flight[way] = send(
                    self.sums.at[chunk], self.full.at[way, s - 1], to
                )

        def finish(self):
            for copy in self.flight:
                copy.wait_recv()
            last = self.size // 2 - 2
            return self.sums[self.at] + self.full[0, last] + self.full[1, last]

    ring_z = Ring(sum_z, half_z, full_z, z, NZ, lambda d: device(dz=d + NZ))
    ring_y = Ring(sum_y, half_y, full_y, y, NY, lambda d: device(dy=d + NY))
    ring_x = Ring(sum_x, half_x, full_x, x, NX, lambda d: device(dx=d + NX))

    def spread(part, got, at, size, hop):
        order = sorted(range(1, size), key=lambda k: -min(k, size - k))
        return [
            send(part.at[(at + k) % size], got.at[k - 1], hop(k)) for k in order
        ]

    def collect(copies, part, got, at, size):
        for copy in copies:
            copy.wait_recv()
        total = part[at]
        for k in range(size - 1):
            total = total + got[k]
        return total

    fills = (fill_z, fill_y, fill_x)
    for p, ring in enumerate((ring_z, ring_y, ring_x)):
        loads[p].wait()
        pairs[p].wait_recv()
        lax.fori_loop(0, NZ, fills[p], 0)
        ring.step(0)
    ring_z.step(1)
    ring_y.step(1)
    ring_x.step(1)
    ring_z.step(2)
    ring_y.step(2)
    mid_x[...] = ring_x.finish()
    second_x = spread(mid_x, got_x, z, NZ, lambda k: device(dz=k))
    ring_z.step(3)
    ring_y.step(3)
    mid_z[...] = ring_z.finish()
    second_z = spread(mid_z, got_z, y, NY, lambda k: device(dy=k))
    done_y = ring_y.finish()
    for k in range(NX):
        mid_y[k] = done_y[:, k // 2, (k % 2) * 4 : (k % 2) * 4 + 4]
    second_y = spread(mid_y, got_y, x, NX, lambda k: device(dx=k))

    end_x[...] = collect(second_x, mid_x, got_x, z, NZ)
    third_x = spread(end_x, last_x, y, NY, lambda k: device(dy=k))
    end_y[...] = collect(second_y, mid_y, got_y, x, NX)
    third_y = spread(end_y, last_y, z, NZ, lambda k: device(dz=k))
    done_z = collect(second_z, mid_z, got_z, y, NY)
    for k in range(NX):
        end_z[k] = done_z[k // 2, (k % 2) * 4 : (k % 2) * 4 + 4]
    third_z = spread(end_z, last_z, x, NX, lambda k: device(dx=k))

    thirds = (
        (third_z, end_z, last_z, x, NX),
        (third_y, end_y, last_y, z, NZ),
        (third_x, end_x, last_x, y, NY),
    )
    for p, third in enumerate(thirds):
        columns = pl.ds(p * LANES, LANES)
        grad_total = collect(*third)
        new_one = beta_one * moment_one[:, columns] + (1.0 - beta_one) * grad_total
        new_two = (
            beta_two * moment_two[:, columns]
            + (1.0 - beta_two) * grad_total * grad_total
        )
        update = new_one / correct_one / (jnp.sqrt(new_two / correct_two) + epsilon)
        old = master[:, columns]
        new_master = old - learn_rate * (update + decay_rate * old)
        total_out[:, columns] = grad_total
        master_out[:, columns] = new_master
        one_out[:, columns] = new_one
        two_out[:, columns] = new_two
        gathered[z, y, c, p] = new_master.astype(jnp.bfloat16)

    far_first = (4, 3, 5, 2, 6, 1, 7)
    other = device(dc=1)
    mine = gathered.at[z, y, c, 0]
    first_z = [send(mine, mine, device(dz=k)) for k in far_first]
    mine = gathered.at[z, y, c, pl.ds(1, 2)]
    first_y = [send(mine, mine, device(dy=k)) for k in far_first]

    def arrived(copy):
        copy.wait_recv()

    for copy in first_z:
        arrived(copy)
    line = gathered.at[:, y, c, 0]
    next_y = [send(line, line, device(dy=k)) for k in far_first]
    send(line, line, other)
    for copy in first_y:
        arrived(copy)
    line = gathered.at[z, :, c, pl.ds(1, 2)]
    next_z = [send(line, line, device(dz=k)) for k in far_first]
    send(line, line, other)
    last = len(taken)
    for k, copy in reversed(list(zip(far_first, next_y))):
        arrived(copy)
        line = gathered.at[:, (y + NY - k) % NY, c, 0]
        send(line, line, other)
    for k, copy in reversed(list(zip(far_first, next_z))):
        arrived(copy)
        line = gathered.at[(z + NZ - k) % NZ, :, c, pl.ds(1, 2)]
        send(line, line, other)
    for copy in taken[last - 1 :] + [taken[last - 1 - len(far_first) - 1]]:
        arrived(copy)
    for copy in taken:
        copy.wait_send()
    assert len(taken) == SEMS, len(taken)


def local(grads, master, moment_one, moment_two):
    view = grads.reshape(2, 8, NZ, NY, NC, PARTS, LANES).transpose(0, 2, 3, 4, 5, 1, 6)
    f32, bf16 = jnp.float32, jnp.bfloat16
    block = jax.ShapeDtypeStruct(master.shape, f32)
    vmem = pl.BlockSpec(memory_space=pltpu.VMEM)
    outs = pl.pallas_call(
        kernel,
        out_shape=(block,) * 4
        + (jax.ShapeDtypeStruct((NZ, NY, NC, PARTS, 4, LANES), bf16),),
        in_specs=[pl.BlockSpec(memory_space=pl.ANY), vmem, vmem, vmem],
        out_specs=(vmem,) * 5,
        scratch_shapes=[
            pltpu.VMEM((PARTS, 2, NZ, NY, 8, LANES), bf16),
            pltpu.VMEM((PARTS, 2, NZ, NY, 8, LANES), bf16),
            pltpu.VMEM((NZ, NY, 2, 8, LANES), f32),
            pltpu.VMEM((NY, NZ, 2, 8, LANES), f32),
            pltpu.VMEM((NX, NZ, NY, 4, LANES), f32),
            pltpu.VMEM((2, NY // 2, 2, 8, LANES), f32),
            pltpu.VMEM((2, NZ // 2 - 1, NY, 2, 8, LANES), f32),
            pltpu.VMEM((2, NZ // 2, 2, 8, LANES), f32),
            pltpu.VMEM((2, NY // 2 - 1, NZ, 2, 8, LANES), f32),
            pltpu.VMEM((2, NZ // 2, NY, 4, LANES), f32),
            pltpu.VMEM((2, NX // 2 - 1, NZ, NY, 4, LANES), f32),
            pltpu.VMEM((NY, 2, 8, LANES), f32),
            pltpu.VMEM((NX, NZ, 4, LANES), f32),
            pltpu.VMEM((NZ, NY, 4, LANES), f32),
            pltpu.VMEM((NY - 1, 2, 8, LANES), f32),
            pltpu.VMEM((NX - 1, NZ, 4, LANES), f32),
            pltpu.VMEM((NZ - 1, NY, 4, LANES), f32),
            pltpu.VMEM((NX, 4, LANES), f32),
            pltpu.VMEM((NZ, 4, LANES), f32),
            pltpu.VMEM((NY, 4, LANES), f32),
            pltpu.VMEM((NX - 1, 4, LANES), f32),
            pltpu.VMEM((NZ - 1, 4, LANES), f32),
            pltpu.VMEM((NY - 1, 4, LANES), f32),
            pltpu.SemaphoreType.DMA((PARTS,)),
            pltpu.SemaphoreType.DMA((SEMS,)),
            pltpu.SemaphoreType.DMA((SEMS,)),
        ],
        compiler_params=pltpu.CompilerParams(collective_id=0, has_side_effects=True),
    )(view, master, moment_one, moment_two)
    secondary = outs[4].transpose(4, 0, 1, 2, 3, 5).reshape(master.shape[0], -1)
    return (*outs[:4], secondary)


def solution(mesh):
    return jax.shard_map(
        local,
        mesh=mesh,
        in_specs=(
            P("hst", "local", None, None),
            P("local", "hst"),
            P("local", "hst"),
            P("local", "hst"),
        ),
        out_specs=(
            P("local", "hst"),
            P("local", "hst"),
            P("local", "hst"),
            P("local", "hst"),
            P("local", None),
        ),
        check_vma=False,
    )
```

time: 123 us -> 63.3 us (0.51)
  blocking collectives: 118 us -> 0 us
  Pallas kernels: 0 us -> 55.2 us
  local copies, waits for them, and re-layouts: 2.5 us -> 7.01 us
  other arithmetic: 1.59 us -> 0 us
    all_to_all x2 -> x0, blocking collectives: 69.1 us -> none  [the longest x1 48.3 us: local(): lax.all_to_all(partial_sum.reshape(row_block, host_count, col_block), 'hs...]
    pallas_call x0 -> x1, Pallas kernels: none -> 55.2 us  [local(): pl.pallas_call(kernel, out_shape=(block,) * 4 + (jax.ShapeDtypeStruct((NZ...]
    all_gather x1 -> x0, blocking collectives: 48.7 us -> none  [local(): lax.all_gather(new_master.astype(jnp.bfloat16), 'hst', axis=1, tiled=True)]
    unnamed x9 -> x5, local copies, waits for them, and re-layouts: 0.77 us -> 7.01 us
    another operation x1 -> x0, local copies, waits for them, and re-layouts: 1.73 us -> none  [local(): gradient.reshape(local_count, row_block, total_cols)]
where the time goes in v1:
time: 63.3 us; the launch traced here: 62.9 us
  Pallas kernels  55.2 us (87%)
  local copies, waits for them, and re-layouts  7.01 us (11%)
  between operations  0.64 us (1%)
    pallas_call x1, Pallas kernels, local(): pl.pallas_call(kernel, out_shape=(block,) * 4 + (jax.ShapeDtypeStruct((NZ...  55.2 us
    unnamed x5, local copies, waits for them, and re-layouts  7.01 us

profile of v1, /device:TPU:1, one launch (start us, length us, event | category | flops | bytes accessed | tf_op | source)
XLA Modules:
  0.0 62.9 jit_solution(4332876760243138257)
XLA Ops:
  0.6 55.2 %shard_map.83 = (f32[4,384]{1,0:T(4,128)}, f32[4,384]{1,0:T(4,128)}, f32[4,384]{1,0:T(4,128)}, f32[4,384]{1,0:T(4,128)}, bf16[8,8,2,3,4,128]{5,4,3,2,1,0:T(4,128)(2,1)}) custom-call(bf16[2,8,8,2,3,8,128]{6,5,4,3,2,1,0:T(8,128)(2,1)} %bitcast.6, f32[4,384]{1,0:T(4,128)} %master.1, f32[4,384]{1,0:T(4,128)} %moment_one.1, f32[4,384]{1,0:T(4,128)} %moment_two.1), custom_call_target="tpu_custom_call" | custom-call | tf_op jit(solution)/shard_map/pallas_call | solution.py:276
  55.9 1.3 %copy.14 = f32[4,384]{1,0:T(4,128)} copy(f32[4,384]{1,0:T(4,128)} %get-tuple-element.20) | data formatting | bytes 12288
  57.2 1.3 %copy.15 = f32[4,384]{1,0:T(4,128)} copy(f32[4,384]{1,0:T(4,128)} %get-tuple-element.21) | data formatting | bytes 12288
  58.5 1.3 %copy.16 = f32[4,384]{1,0:T(4,128)} copy(f32[4,384]{1,0:T(4,128)} %get-tuple-element.22) | data formatting | bytes 12288
  59.7 1.3 %copy.17 = f32[4,384]{1,0:T(4,128)} copy(f32[4,384]{1,0:T(4,128)} %get-tuple-element.23) | data formatting | bytes 12288
  61.0 1.9 %copy.18 = bf16[4,49152]{1,0:T(4,128)(2,1)} copy(bf16[4,49152]{1,0:T(4,128)(2,1)} %bitcast.7) | data formatting | bytes 786432

commit v2 on v1

--- a/solution.py
+++ b/solution.py
@@ -26,11 +26,10 @@
     master,
     moment_one,
     moment_two,
-    total_out,
-    master_out,
-    one_out,
-    two_out,
+    packed_out,
     gathered,
+    states,
+    packed,
     own,
     peer,
     sum_z,
@@ -54,6 +53,8 @@
     last_z,
     last_y,
     last_x,
+    state_sem,
+    pack_sem,
     load_sem,
     send_sem,
     recv_sem,
@@ -96,6 +97,11 @@
         )
         load.start()
         loads.append(load)
+    state_loads = []
+    for k, ref in enumerate((master, moment_one, moment_two)):
+        load = pltpu.make_async_copy(ref, states.at[k], state_sem.at[k])
+        load.start()
+        state_loads.append(load)
     pl.semaphore_wait(barrier, len(peers))
 
     pairs = [
@@ -215,21 +221,23 @@
         (third_y, end_y, last_y, z, NZ),
         (third_x, end_x, last_x, y, NY),
     )
+    for load in state_loads:
+        load.wait()
     for p, third in enumerate(thirds):
         columns = pl.ds(p * LANES, LANES)
         grad_total = collect(*third)
-        new_one = beta_one * moment_one[:, columns] + (1.0 - beta_one) * grad_total
+        new_one = beta_one * states[1, :, columns] + (1.0 - beta_one) * grad_total
         new_two = (
-            beta_two * moment_two[:, columns]
+            beta_two * states[2, :, columns]
             + (1.0 - beta_two) * grad_total * grad_total
         )
         update = new_one / correct_one / (jnp.sqrt(new_two / correct_two) + epsilon)
-        old = master[:, columns]
+        old = states[0, :, columns]
         new_master = old - learn_rate * (update + decay_rate * old)
-        total_out[:, columns] = grad_total
-        master_out[:, columns] = new_master
-        one_out[:, columns] = new_one
-        two_out[:, columns] = new_two
+        packed[0, :, columns] = grad_total
+        packed[1, :, columns] = new_master
+        packed[2, :, columns] = new_one
+        packed[3, :, columns] = new_two
         gathered[z, y, c, p] = new_master.astype(jnp.bfloat16)
 
     far_first = (4, 3, 5, 2, 6, 1, 7)
@@ -239,6 +247,9 @@
     mine = gathered.at[z, y, c, pl.ds(1, 2)]
     first_y = [send(mine, mine, device(dy=k)) for k in far_first]
 
+    pack = pltpu.make_async_copy(packed, packed_out, pack_sem)
+    pack.start()
+
     def arrived(copy):
         copy.wait_recv()
 
@@ -265,21 +276,44 @@
         arrived(copy)
     for copy in taken:
         copy.wait_send()
+    pack.wait()
     assert len(taken) == SEMS, len(taken)
+
+
+def finish(packed, gathered, *refs):
+    outs, (states, weights, load_sem, store_sem) = refs[:5], refs[5:]
+    first = pltpu.make_async_copy(gathered, weights, load_sem.at[0])
+    second = pltpu.make_async_copy(packed, states, load_sem.at[1])
+    first.start()
+    second.start()
+    first.wait()
+    stores = [pltpu.make_async_copy(weights, outs[4], store_sem.at[4])]
+    stores[0].start()
+    second.wait()
+    for k in range(4):
+        store = pltpu.make_async_copy(states.at[k], outs[k], store_sem.at[k])
+        store.start()
+        stores.append(store)
+    for store in stores:
+        store.wait()
 
 
 def local(grads, master, moment_one, moment_two):
     view = grads.reshape(2, 8, NZ, NY, NC, PARTS, LANES).transpose(0, 2, 3, 4, 5, 1, 6)
     f32, bf16 = jnp.float32, jnp.bfloat16
     block = jax.ShapeDtypeStruct(master.shape, f32)
+    block_all = jax.ShapeDtypeStruct((4,) + master.shape, f32)
+    weights = jax.ShapeDtypeStruct((NZ, NY, NC, PARTS, 4, LANES), bf16)
     vmem = pl.BlockSpec(memory_space=pltpu.VMEM)
-    outs = pl.pallas_call(
+    hbm = pl.BlockSpec(memory_space=pl.ANY)
+    packed, gathered = pl.pallas_call(
         kernel,
-        out_shape=(block,) * 4
-        + (jax.ShapeDtypeStruct((NZ, NY, NC, PARTS, 4, LANES), bf16),),
-        in_specs=[pl.BlockSpec(memory_space=pl.ANY), vmem, vmem, vmem],
-        out_specs=(vmem,) * 5,
+        out_shape=(block_all, weights),
+        in_specs=[hbm] * 4,
+        out_specs=(hbm, vmem),
         scratch_shapes=[
+            pltpu.VMEM((3,) + master.shape, f32),
+            pltpu.VMEM((4,) + master.shape, f32),
             pltpu.VMEM((PARTS, 2, NZ, NY, 8, LANES), bf16),
             pltpu.VMEM((PARTS, 2, NZ, NY, 8, LANES), bf16),
             pltpu.VMEM((NZ, NY, 2, 8, LANES), f32),
@@ -303,12 +337,26 @@
             pltpu.VMEM((NX - 1, 4, LANES), f32),
             pltpu.VMEM((NZ - 1, 4, LANES), f32),
             pltpu.VMEM((NY - 1, 4, LANES), f32),
+            pltpu.SemaphoreType.DMA((3,)),
+            pltpu.SemaphoreType.DMA,
             pltpu.SemaphoreType.DMA((PARTS,)),
             pltpu.SemaphoreType.DMA((SEMS,)),
             pltpu.SemaphoreType.DMA((SEMS,)),
         ],
         compiler_params=pltpu.CompilerParams(collective_id=0, has_side_effects=True),
     )(view, master, moment_one, moment_two)
+    outs = pl.pallas_call(
+        finish,
+        out_shape=(block,) * 4 + (weights,),
+        in_specs=[hbm] * 2,
+        out_specs=(hbm,) * 5,
+        scratch_shapes=[
+            pltpu.VMEM(block_all.shape, f32),
+            pltpu.VMEM(weights.shape, bf16),
+            pltpu.SemaphoreType.DMA((2,)),
+            pltpu.SemaphoreType.DMA((5,)),
+        ],
+    )(packed, gathered)
     secondary = outs[4].transpose(4, 0, 1, 2, 3, 5).reshape(master.shape[0], -1)
     return (*outs[:4], secondary)
 

time: 63.3 us -> 57.4 us (0.907)
  local copies, waits for them, and re-layouts: 7.01 us -> 0 us
  Pallas kernels: 55.2 us -> 56.6 us
    unnamed x5 -> x0, local copies, waits for them, and re-layouts: 7.01 us -> none
    pallas_call x1 -> x2, Pallas kernels: 55.2 us -> 56.6 us  [the longest x1 54.8 us: local(): pl.pallas_call(kernel, out_shape=(block_all, weights), in_specs=[hbm] * 4...]
where the time goes in v2:
time: 57.4 us; the launch traced here: 57.2 us
  Pallas kernels  56.6 us (99%)
  between operations  0.64 us (1%)
    pallas_call x1, Pallas kernels, local(): pl.pallas_call(kernel, out_shape=(block_all, weights), in_specs=[hbm] * 4...  54.8 us
    pallas_call x1, Pallas kernels, local(): pl.pallas_call(finish, out_shape=(block,) * 4 + (weights,), in_specs=[hbm...  1.81 us

profile of v2, /device:TPU:1, one launch (start us, length us, event | category | flops | bytes accessed | tf_op | source)
XLA Modules:
  0.0 57.2 jit_solution(9068406140045312858)
XLA Ops:
  0.6 54.8 %shard_map.83 = (f32[4,4,384]{2,1,0:T(4,128)}, bf16[8,8,2,3,4,128]{5,4,3,2,1,0:T(4,128)(2,1)}) custom-call(bf16[2,8,8,2,3,8,128]{6,5,4,3,2,1,0:T(8,128)(2,1)} %bitcast.6, f32[4,384]{1,0:T(4,128)} %master.1, f32[4,384]{1,0:T(4,128)} %moment_one.1, f32[4,384]{1,0:T(4,128)} %moment_two.1), custom_call_target="tpu_custom_call" | custom-call | tf_op jit(solution)/shard_map/pallas_call | solution.py:309
  55.4 1.8 %shard_map.84 = (f32[4,384]{1,0:T(4,128)}, f32[4,384]{1,0:T(4,128)}, f32[4,384]{1,0:T(4,128)}, f32[4,384]{1,0:T(4,128)}, bf16[8,8,2,3,4,128]{5,4,3,2,1,0:T(4,128)(2,1)}) custom-call(f32[4,4,384]{2,1,0:T(4,128)} %get-tuple-element.12.packed, bf16[8,8,2,3,4,128]{5,4,3,2,1,0:T(4,128)(2,1)} %get-tuple-element.13.gathered), custom_call_target="tpu_custom_call" | custom-call | tf_op jit(solution)/shard_map/pallas_call | solution.py:348

commit v3 on v2

--- a/solution.py
+++ b/solution.py
@@ -85,9 +85,9 @@
 
     barrier = pltpu.get_barrier_semaphore()
     peers = [device(dc=1)]
-    peers += [device(dx=k) for k in range(1, NX)]
-    peers += [device(dy=k) for k in range(1, NY)]
-    peers += [device(dz=k) for k in range(1, NZ)]
+    peers += [device(dx=k) for k in (1, NX - 1)]
+    peers += [device(dy=k) for k in (1, NY - 1)]
+    peers += [device(dz=k) for k in (1, NZ - 1)]
     for to in peers:
         pl.semaphore_signal(barrier, inc=1, device_id=to, device_id_type=MESH)
     loads = []
@@ -171,8 +171,9 @@
     ring_y = Ring(sum_y, half_y, full_y, y, NY, lambda d: device(dy=d + NY))
     ring_x = Ring(sum_x, half_x, full_x, x, NX, lambda d: device(dx=d + NX))
 
-    def spread(part, got, at, size, hop):
-        order = sorted(range(1, size), key=lambda k: -min(k, size - k))
+    def spread(part, got, at, size, hop, order=None):
+        if order is None:
+            order = sorted(range(1, size), key=lambda k: -min(k, size - k))
         return [
             send(part.at[(at + k) % size], got.at[k - 1], hop(k)) for k in order
         ]
@@ -197,12 +198,17 @@
     ring_z.step(2)
     ring_y.step(2)
     mid_x[...] = ring_x.finish()
-    second_x = spread(mid_x, got_x, z, NZ, lambda k: device(dz=k))
     ring_z.step(3)
     ring_y.step(3)
+
+    def start_x(order):
+        return spread(mid_x, got_x, z, NZ, lambda k: device(dz=k), order)
+
+    second_x = start_x((3, 5, 2, 6, 1, 7))
     mid_z[...] = ring_z.finish()
+    second_x += start_x((4,))
+    done_y = ring_y.finish()
     second_z = spread(mid_z, got_z, y, NY, lambda k: device(dy=k))
-    done_y = ring_y.finish()
     for k in range(NX):
         mid_y[k] = done_y[:, k // 2, (k % 2) * 4 : (k % 2) * 4 + 4]
     second_y = spread(mid_y, got_y, x, NX, lambda k: device(dx=k))

time: 57.4 us -> 55 us (0.958)
  Pallas kernels: 56.6 us -> 54.2 us
    pallas_call x1, Pallas kernels: 54.8 us -> 52.4 us  [local(): pl.pallas_call(kernel, out_shape=(block_all, weights), in_specs=[hbm] * 4...]
where the time goes in v3:
time: 55 us; the launch traced here: 54.8 us
  Pallas kernels  54.2 us (99%)
  between operations  0.64 us (1%)
    pallas_call x1, Pallas kernels, local(): pl.pallas_call(kernel, out_shape=(block_all, weights), in_specs=[hbm] * 4...  52.4 us
    pallas_call x1, Pallas kernels, local(): pl.pallas_call(finish, out_shape=(block,) * 4 + (weights,), in_specs=[hbm...  1.81 us

profile of v3, /device:TPU:1, one launch (start us, length us, event | category | flops | bytes accessed | tf_op | source)
XLA Modules:
  0.0 54.8 jit_solution(31753569580445634)
XLA Ops:
  0.6 52.4 %shard_map.83 = (f32[4,4,384]{2,1,0:T(4,128)}, bf16[8,8,2,3,4,128]{5,4,3,2,1,0:T(4,128)(2,1)}) custom-call(bf16[2,8,8,2,3,8,128]{6,5,4,3,2,1,0:T(8,128)(2,1)} %bitcast.6, f32[4,384]{1,0:T(4,128)} %master.1, f32[4,384]{1,0:T(4,128)} %moment_one.1, f32[4,384]{1,0:T(4,128)} %moment_two.1), custom_call_target="tpu_custom_call" | custom-call | tf_op jit(solution)/shard_map/pallas_call | solution.py:315
  53.0 1.8 %shard_map.84 = (f32[4,384]{1,0:T(4,128)}, f32[4,384]{1,0:T(4,128)}, f32[4,384]{1,0:T(4,128)}, f32[4,384]{1,0:T(4,128)}, bf16[8,8,2,3,4,128]{5,4,3,2,1,0:T(4,128)(2,1)}) custom-call(f32[4,4,384]{2,1,0:T(4,128)} %get-tuple-element.12.packed, bf16[8,8,2,3,4,128]{5,4,3,2,1,0:T(4,128)(2,1)} %get-tuple-element.13.gathered), custom_call_target="tpu_custom_call" | custom-call | tf_op jit(solution)/shard_map/pallas_call | solution.py:354

commit v4 on v3

--- a/solution.py
+++ b/solution.py
@@ -18,7 +18,7 @@
 NX, NY, NZ, NC = 4, 8, 8, 2
 PARTS, LANES = 3, 128
 MESH = pl.DeviceIdType.MESH
-SEMS = 101
+SEMS = 115
 
 
 def kernel(
@@ -138,31 +138,48 @@
         def __init__(self, sums, half, full, at, size, hop):
             self.sums, self.half, self.full = sums, half, full
             self.at, self.size, self.hop = at, size, hop
-            self.flight = [None, None]
+            self.cut = sums.shape[1] // 2
+            self.first = [None, None]
+            self.flight = [[None, None], [None, None]]
+
+        def chunk(self, way, s):
+            away = self.size // 2 - s
+            return (self.at + self.size + (away if way == 0 else -away)) % self.size
+
+        def push(self, way, s, sub):
+            part = pl.ds(sub * self.cut, self.cut)
+            src = self.sums.at[self.chunk(way, s), part]
+            to = self.hop(1 if way == 0 else -1)
+            if s == 0:
+                self.first[way] = send(src, self.half.at[way], to)
+            else:
+                dst = self.full.at[way, s - 1, part]
+                self.flight[way][sub] = send(src, dst, to)
+
+        def start(self):
+            for way in range(2):
+                self.push(way, 0, way)
+            for way in range(2):
+                self.push(way, 1, 1 - way)
 
         def step(self, s):
-            far = self.size // 2
-            cut = self.sums.shape[1] // 2
-            for way, sign in enumerate((1, -1)):
-                to = self.hop(sign)
-                chunk = (self.at + self.size + sign * (far - s)) % self.size
-                lo = way * cut
-                if s == 0:
-                    self.flight[way] = send(
-                        self.sums.at[chunk, pl.ds(lo, cut)], self.half.at[way], to
-                    )
-                    continue
-                self.flight[way].wait_recv()
-                if s == 1:
-                    self.sums[chunk, pl.ds(lo, cut)] += self.half[way]
-                else:
-                    self.sums[chunk] += self.full[way, s - 2]
-                self.flight[way] = send(
-                    self.sums.at[chunk], self.full.at[way, s - 1], to
-                )
+            for turn in range(2):
+                for way in range(2):
+                    sub = way if turn else 1 - way
+                    part = pl.ds(sub * self.cut, self.cut)
+                    if s == 1:
+                        if turn == 0:
+                            continue
+                        self.first[way].wait_recv()
+                        got = self.half[way]
+                    else:
+                        self.flight[way][sub].wait_recv()
+                        got = self.full[way, s - 2, part]
+                    self.sums[self.chunk(way, s), part] += got
+                    self.push(way, s, sub)
 
         def finish(self):
-            for copy in self.flight:
+            for copy in self.flight[0] + self.flight[1]:
                 copy.wait_recv()
             last = self.size // 2 - 2
             return self.sums[self.at] + self.full[0, last] + self.full[1, last]
@@ -191,7 +208,7 @@
         loads[p].wait()
         pairs[p].wait_recv()
         lax.fori_loop(0, NZ, fills[p], 0)
-        ring.step(0)
+        ring.start()
     ring_z.step(1)
     ring_y.step(1)
     ring_x.step(1)
@@ -227,6 +244,7 @@
         (third_y, end_y, last_y, z, NZ),
         (third_x, end_x, last_x, y, NY),
     )
+    far_first = (4, 3, 5, 2, 6, 1, 7)
     for load in state_loads:
         load.wait()
     for p, third in enumerate(thirds):
@@ -245,11 +263,11 @@
         packed[2, :, columns] = new_one
         packed[3, :, columns] = new_two
         gathered[z, y, c, p] = new_master.astype(jnp.bfloat16)
-
-    far_first = (4, 3, 5, 2, 6, 1, 7)
+        if p == 0:
+            mine = gathered.at[z, y, c, 0]
+            first_z = [send(mine, mine, device(dz=k)) for k in far_first]
+
     other = device(dc=1)
-    mine = gathered.at[z, y, c, 0]
-    first_z = [send(mine, mine, device(dz=k)) for k in far_first]
     mine = gathered.at[z, y, c, pl.ds(1, 2)]
     first_y = [send(mine, mine, device(dy=k)) for k in far_first]
 

time: 55 us -> 55.5 us (level)
  no operation moved by 1% of the time
where the time goes in v4:
time: 55.5 us; the launch traced here: 55.4 us
  Pallas kernels  54.7 us (99%)
  between operations  0.64 us (1%)
    pallas_call x1, Pallas kernels, local(): pl.pallas_call(kernel, out_shape=(block_all, weights), in_specs=[hbm] * 4...  52.9 us
    pallas_call x1, Pallas kernels, local(): pl.pallas_call(finish, out_shape=(block,) * 4 + (weights,), in_specs=[hbm...  1.81 us

profile of v4, /device:TPU:1, one launch (start us, length us, event | category | flops | bytes accessed | tf_op | source)
XLA Modules:
  0.0 55.4 jit_solution(5780373535605941584)
XLA Ops:
  0.6 52.9 %shard_map.83 = (f32[4,4,384]{2,1,0:T(4,128)}, bf16[8,8,2,3,4,128]{5,4,3,2,1,0:T(4,128)(2,1)}) custom-call(bf16[2,8,8,2,3,8,128]{6,5,4,3,2,1,0:T(8,128)(2,1)} %bitcast.6, f32[4,384]{1,0:T(4,128)} %master.1, f32[4,384]{1,0:T(4,128)} %moment_one.1, f32[4,384]{1,0:T(4,128)} %moment_two.1), custom_call_target="tpu_custom_call" | custom-call | tf_op jit(solution)/shard_map/pallas_call | solution.py:333
  53.5 1.8 %shard_map.84 = (f32[4,384]{1,0:T(4,128)}, f32[4,384]{1,0:T(4,128)}, f32[4,384]{1,0:T(4,128)}, f32[4,384]{1,0:T(4,128)}, bf16[8,8,2,3,4,128]{5,4,3,2,1,0:T(4,128)(2,1)}) custom-call(f32[4,4,384]{2,1,0:T(4,128)} %get-tuple-element.12.packed, bf16[8,8,2,3,4,128]{5,4,3,2,1,0:T(4,128)(2,1)} %get-tuple-element.13.gathered), custom_call_target="tpu_custom_call" | custom-call | tf_op jit(solution)/shard_map/pallas_call | solution.py:372

commit v5 on v4

--- a/solution.py
+++ b/solution.py
@@ -274,30 +274,55 @@
     pack = pltpu.make_async_copy(packed, packed_out, pack_sem)
     pack.start()
 
-    def arrived(copy):
+    def line_copy(slot, ref, to):
+        return pltpu.make_async_remote_copy(
+            src_ref=ref,
+            dst_ref=ref,
+            send_sem=send_sem.at[slot],
+            recv_sem=recv_sem.at[slot],
+            device_id=to,
+            device_id_type=MESH,
+        )
+
+    line_y = gathered.at[:, y, c, 0]
+    line_z = gathered.at[z, :, c, pl.ds(1, 2)]
+    next_y, next_z = [], []
+    for nexts, line, hop in (
+        (next_y, line_y, lambda k: device(dy=k)),
+        (next_z, line_z, lambda k: device(dz=k)),
+    ):
+        for k in far_first:
+            copy = line_copy(len(taken), line, hop(k))
+            nexts.append((len(taken), k, copy))
+            taken.append(copy)
+
+    def pass_y(k):
+        piece = gathered.at[(z + NZ - k) % NZ, y, c, 0]
+        for slot, far, _ in next_y:
+            line_copy(slot, piece, device(dy=far)).start()
+
+    def pass_z(k):
+        piece = gathered.at[z, (y + NY - k) % NY, c, pl.ds(1, 2)]
+        for slot, far, _ in next_z:
+            line_copy(slot, piece, device(dz=far)).start()
+
+    pass_y(0)
+    pass_z(0)
+    for k, copy_z, copy_y in reversed(list(zip(far_first, first_z, first_y))):
+        copy_z.wait_recv()
+        pass_y(k)
+        copy_y.wait_recv()
+        pass_z(k)
+    across = [send(line_y, line_y, other), send(line_z, line_z, other)]
+    for (_, k, copy_y), (_, _, copy_z) in reversed(list(zip(next_y, next_z))):
+        copy_y.wait_recv()
+        line = gathered.at[:, (y + NY - k) % NY, c, 0]
+        across.append(send(line, line, other))
+        copy_z.wait_recv()
+        line = gathered.at[(z + NZ - k) % NZ, :, c, pl.ds(1, 2)]
+        across.append(send(line, line, other))
+    for copy in across:
         copy.wait_recv()
-
-    for copy in first_z:
-        arrived(copy)
-    line = gathered.at[:, y, c, 0]
-    next_y = [send(line, line, device(dy=k)) for k in far_first]
-    send(line, line, other)
-    for copy in first_y:
-        arrived(copy)
-    line = gathered.at[z, :, c, pl.ds(1, 2)]
-    next_z = [send(line, line, device(dz=k)) for k in far_first]
-    send(line, line, other)
-    last = len(taken)
-    for k, copy in reversed(list(zip(far_first, next_y))):
-        arrived(copy)
-        line = gathered.at[:, (y + NY - k) % NY, c, 0]
-        send(line, line, other)
-    for k, copy in reversed(list(zip(far_first, next_z))):
-        arrived(copy)
-        line = gathered.at[(z + NZ - k) % NZ, :, c, pl.ds(1, 2)]
-        send(line, line, other)
-    for copy in taken[last - 1 :] + [taken[last - 1 - len(far_first) - 1]]:
-        arrived(copy)
     for copy in taken:
         copy.wait_send()
     pack.wait()

time: 55.5 us -> 54.3 us (0.978)
  Pallas kernels: 54.7 us -> 53.5 us
    pallas_call x1, Pallas kernels: 52.9 us -> 51.7 us  [local(): pl.pallas_call(kernel, out_shape=(block_all, weights), in_specs=[hbm] * 4...]
where the time goes in v5:
time: 54.3 us; the launch traced here: 54.1 us
  Pallas kernels  53.5 us (99%)
  between operations  0.64 us (1%)
    pallas_call x1, Pallas kernels, local(): pl.pallas_call(kernel, out_shape=(block_all, weights), in_specs=[hbm] * 4...  51.7 us
    pallas_call x1, Pallas kernels, local(): pl.pallas_call(finish, out_shape=(block,) * 4 + (weights,), in_specs=[hbm...  1.81 us

profile of v5, /device:TPU:1, one launch (start us, length us, event | category | flops | bytes accessed | tf_op | source)
XLA Modules:
  0.0 54.1 jit_solution(11411960730702002114)
XLA Ops:
  0.6 51.7 %shard_map.83 = (f32[4,4,384]{2,1,0:T(4,128)}, bf16[8,8,2,3,4,128]{5,4,3,2,1,0:T(4,128)(2,1)}) custom-call(bf16[2,8,8,2,3,8,128]{6,5,4,3,2,1,0:T(8,128)(2,1)} %bitcast.6, f32[4,384]{1,0:T(4,128)} %master.1, f32[4,384]{1,0:T(4,128)} %moment_one.1, f32[4,384]{1,0:T(4,128)} %moment_two.1), custom_call_target="tpu_custom_call" | custom-call | tf_op jit(solution)/shard_map/pallas_call | solution.py:358
  52.3 1.8 %shard_map.84 = (f32[4,384]{1,0:T(4,128)}, f32[4,384]{1,0:T(4,128)}, f32[4,384]{1,0:T(4,128)}, f32[4,384]{1,0:T(4,128)}, bf16[8,8,2,3,4,128]{5,4,3,2,1,0:T(4,128)(2,1)}) custom-call(f32[4,4,384]{2,1,0:T(4,128)} %get-tuple-element.12.packed, bf16[8,8,2,3,4,128]{5,4,3,2,1,0:T(4,128)(2,1)} %get-tuple-element.13.gathered), custom_call_target="tpu_custom_call" | custom-call | tf_op jit(solution)/shard_map/pallas_call | solution.py:397
